TPU v7x, 32 devices: a whole 2x2x4 slice. The times are simulated.
32 devices in a mesh: dp: 16 (over z, x, core), tensor: 2 (over y).
Axes of the slice: x: 2, y: 2, z: 4, core: 2. Of those that a mesh axis runs over, the one named last changes fastest.
Arguments:
- x_in: bfloat16 [16384, 2048], P('dp'), may hold values from -6 to 6
- norm_gain: float32 [2048], replicated, may hold values from 0.5 to 1.5
- w_zx: bfloat16 [2048, 2, 4096], P(None, None, 'tensor'), may hold values from -0.125 to 0.125
- w_bc: bfloat16 [2048, 256], replicated, may hold values from -0.125 to 0.125
- w_dt: bfloat16 [2048, 64], P(None, 'tensor'), may hold values from -0.125 to 0.125
- conv_x: float32 [5, 4096], P(None, 'tensor'), may hold values from -3 to 3
- conv_bc: float32 [5, 256], replicated, may hold values from -3 to 3
- dt_bias: float32 [64], P('tensor'), may hold values from -4 to -1
- a_log: float32 [64], P('tensor'), may hold values from -3 to 1.5
- d_skip: float32 [64], P('tensor'), may hold values from 0.5 to 1.5
- gate_gain: float32 [4096], P('tensor'), may hold values from 0.5 to 1.5
- w_out: bfloat16 [4096, 2048], P('tensor'), may hold values from -0.09375 to 0.09375
- cotangent: bfloat16 [16384, 2048], P('dp'), may hold values from -6 to 6
- block_parent: int32 [128], P('dp'), may hold values from -1 to 6, as said below
Outputs:
- mixed: bfloat16 [16384, 2048], P('dp')
- input_grad: bfloat16 [16384, 2048], P('dp')
- norm_gain_grad: float32 [2048], replicated
- w_zx_grad: float32 [2048, 2, 4096], P('dp', None, 'tensor')
- w_bc_grad: float32 [2048, 256], replicated
- w_dt_grad: float32 [2048, 64], P('dp', 'tensor')
- conv_x_grad: float32 [5, 4096], P(None, 'tensor')
- conv_bc_grad: float32 [5, 256], replicated
- dt_bias_grad: float32 [64], P('tensor')
- a_log_grad: float32 [64], P('tensor')
- d_skip_grad: float32 [64], P('tensor')
- gate_gain_grad: float32 [4096], P('tensor')
- w_out_grad: float32 [4096, 2048], P('tensor', 'dp')
Inputs may be any that keep to these rules, and one draw needn't show every extreme that they name: `block_parent`: each device's 8 blocks hold one tree. A block's entry is the index, among its device's blocks, of an earlier block whose last token precedes its first token, or -1 at the root; the first half of the blocks or more form a chain from the root, and the last block continues the block before it.
All inputs are finite; a program needn't handle non-finite values.
Results may differ from a plain program's by a relative error of at most 0.014.
Values may be sent and summed in bfloat16 or wider, within the bound.
No kernel may reach another device: no remote copies, remote signals or barrier semaphores. Data moves between devices by JAX's collectives and lax.ppermute only.
A program may use at most 320 MiB of HBM per device.

v0:
```python
import jax
import jax.numpy as jnp
from jax import lax
from jax.sharding import PartitionSpec as P

epsilon = 1e-05
highest = lax.Precision.HIGHEST


def conv_path(inputs, kernel, parent):
    blocks = parent.shape[0]
    tokens, channels = inputs.shape
    window = kernel.shape[0] - 1
    block_len = tokens // blocks
    blocked = inputs.reshape(blocks, block_len, channels)
    trailing = blocked[:, block_len - (window - 1) :, :]
    context = jnp.take(trailing, jnp.maximum(parent, 0), axis=0)
    context = jnp.where((parent >= 0)[:, None, None], context, jnp.zeros_like(context))
    padded = jnp.concatenate([context, blocked], axis=1)
    summed = kernel[window][None, None, :] + jnp.zeros_like(blocked)
    for offset in range(window):
        summed = summed + kernel[offset][None, None, :] * padded[:, offset : offset + block_len, :]
    return jax.nn.silu(summed).reshape(tokens, channels)


def decay_paths(block_decay, parent):
    blocks = parent.shape[0]
    n_heads = block_decay.shape[1]
    parent_map = (parent[:, None] == jnp.arange(blocks, dtype=jnp.int32)[None, :]).astype(
        jnp.float32
    )
    identity = jnp.eye(blocks, dtype=jnp.float32)

    def advance(turn, paths):
        return identity[None] + jnp.einsum(
            "hb,bp,hpa->hba", block_decay.T, parent_map, paths, precision=highest
        )

    paths = lax.fori_loop(0, blocks, advance, jnp.broadcast_to(identity, (n_heads, blocks, blocks)))
    return (paths, parent_map)


def ssd_mix(x_heads, b_rows, c_rows, dt_raw, dt_bias, a_log, d_skip, parent):
    tokens, n_heads, head_dim = x_heads.shape
    blocks = parent.shape[0]
    block_len = tokens // blocks
    dt_values = jax.nn.softplus(dt_raw + dt_bias)
    log_rate = dt_values * -jnp.exp(a_log)
    x_blocks = x_heads.reshape(blocks, block_len, n_heads, head_dim)
    b_blocks = b_rows.reshape(blocks, block_len, -1)
    c_blocks = c_rows.reshape(blocks, block_len, -1)
    dt_blocks = dt_values.reshape(blocks, block_len, n_heads)
    cumulant = jnp.cumsum(log_rate.reshape(blocks, block_len, n_heads), axis=1)
    scores = jnp.einsum("bin,bjn->bij", c_blocks, b_blocks, precision=highest)
    rows_idx = jnp.arange(block_len, dtype=jnp.int32)
    causal = (rows_idx[:, None] >= rows_idx[None, :])[None, :, :, None]
    log_gap = cumulant[:, :, None, :] - cumulant[:, None, :, :]
    decays = jnp.where(causal, jnp.exp(jnp.where(causal, log_gap, 0.0)), 0.0)
    weights = scores[..., None] * decays * dt_blocks[:, None, :, :]
    within = jnp.einsum("bijh,bjhp->bihp", weights, x_blocks, precision=highest)
    to_end = jnp.exp(cumulant[:, -1:, :] - cumulant) * dt_blocks
    local_states = jnp.einsum("bjh,bjhp,bjn->bhpn", to_end, x_blocks, b_blocks, precision=highest)
    paths, parent_map = decay_paths(jnp.exp(cumulant[:, -1, :]), parent)
    end_states = jnp.einsum("hba,ahpn->bhpn", paths, local_states, precision=highest)
    start_states = jnp.einsum("bq,qhpn->bhpn", parent_map, end_states, precision=highest)
    carried = jnp.exp(cumulant)[..., None] * jnp.einsum(
        "bin,bhpn->bihp", c_blocks, start_states, precision=highest
    )
    result = within + carried + d_skip[None, None, :, None] * x_blocks
    return result.reshape(tokens, n_heads * head_dim)


def gated_mix(x_heads, bc_rows, dt_raw, dt_bias, a_log, d_skip, z_gate, parent):
    half = bc_rows.shape[1] // 2
    mixed_heads = ssd_mix(
        x_heads, bc_rows[:, :half], bc_rows[:, half:], dt_raw, dt_bias, a_log, d_skip, parent
    )
    return mixed_heads * jax.nn.silu(z_gate)


def over_tokens(left, right):
    return lax.dot_general(
        left, right, (((0,), (0,)), ((), ())), preferred_element_type=jnp.float32
    )


def over_columns(left, right):
    return lax.dot_general(
        left, right, (((1,), (1,)), ((), ())), preferred_element_type=jnp.float32
    )


def rounded(value):
    return lax.optimization_barrier(value.astype(jnp.bfloat16)).astype(jnp.float32)


def local(
    x_in,
    norm_gain,
    w_zx,
    w_bc,
    w_dt,
    conv_x,
    conv_bc,
    dt_bias,
    a_log,
    d_skip,
    gate_gain,
    w_out,
    cotangent,
    block_parent,
):
    tokens, features = x_in.shape
    local_heads = w_dt.shape[1]
    inner_width = w_zx.shape[2]
    head_dim = inner_width // local_heads
    full_width = inner_width * lax.axis_size("tensor")
    x_float = x_in.astype(jnp.float32)
    inv_rms = lax.rsqrt(jnp.mean(x_float * x_float, axis=-1) + epsilon)
    normed = (x_float * inv_rms[:, None] * norm_gain).astype(jnp.bfloat16)
    z_gate = jnp.dot(normed, w_zx[:, 0, :], preferred_element_type=jnp.float32)
    x_pre = jnp.dot(normed, w_zx[:, 1, :], preferred_element_type=jnp.float32)
    bc_pre = jnp.dot(normed, w_bc, preferred_element_type=jnp.float32)
    dt_raw = jnp.dot(normed, w_dt, preferred_element_type=jnp.float32)

    def x_piece(values, kernel):
        return conv_path(values, kernel, block_parent)

    x_conv, x_pull = jax.vjp(x_piece, x_pre, conv_x)
    bc_conv, bc_pull = jax.vjp(x_piece, bc_pre, conv_bc)
    x_round = rounded(x_conv)
    bc_round = rounded(bc_conv)

    def mixer(x_values, bc_values, dt_values, bias_values, log_values, skip_values, gate_values):
        return gated_mix(
            x_values.reshape(tokens, local_heads, head_dim),
            bc_values,
            dt_values,
            bias_values,
            log_values,
            skip_values,
            gate_values,
            block_parent,
        )

    gated, mix_pull = jax.vjp(mixer, x_round, bc_round, dt_raw, dt_bias, a_log, d_skip, z_gate)
    squares = lax.psum(jnp.sum(gated * gated, axis=-1), "tensor")
    inv_gate = lax.rsqrt(squares / full_width + epsilon)
    gate_normed = (gated * inv_gate[:, None] * gate_gain).astype(jnp.bfloat16)
    partial_out = jnp.dot(gate_normed, w_out, preferred_element_type=jnp.float32)
    share = tokens // lax.axis_size("tensor")
    first_row = lax.axis_index("tensor") * share
    x_rows = lax.dynamic_slice_in_dim(x_float, first_row, share, 0)
    mixed = (
        x_float + lax.psum(partial_out.astype(jnp.bfloat16), "tensor").astype(jnp.float32)
    ).astype(jnp.bfloat16)
    d_gate_normed = over_columns(cotangent, w_out)
    w_out_part = over_tokens(gate_normed, cotangent)
    gate_gain_part = jnp.sum(d_gate_normed * gated * inv_gate[:, None], axis=0)
    scaled = d_gate_normed * gate_gain
    cross = lax.psum(jnp.sum(scaled * gated, axis=-1), "tensor")
    d_gated = (
        inv_gate[:, None] * scaled
        - gated * (inv_gate * inv_gate * inv_gate * cross / full_width)[:, None]
    )
    d_x_round, d_bc_round, d_dt_raw, dt_bias_part, a_log_part, d_skip_part, d_z_gate = mix_pull(
        d_gated
    )
    d_x_pre, conv_x_part = x_pull(d_x_round)
    d_bc_pre, conv_bc_part = bc_pull(d_bc_round)
    z_low = d_z_gate.astype(jnp.bfloat16)
    x_low = d_x_pre.astype(jnp.bfloat16)
    bc_low = d_bc_pre.astype(jnp.bfloat16)
    dt_low = d_dt_raw.astype(jnp.bfloat16)
    w_zx_part = jnp.stack([over_tokens(normed, z_low), over_tokens(normed, x_low)], axis=1)
    w_bc_part = over_tokens(normed, bc_low)
    w_dt_part = over_tokens(normed, dt_low)
    d_normed = over_columns(z_low, w_zx[:, 0, :]) + over_columns(x_low, w_zx[:, 1, :])
    d_normed = d_normed + over_columns(bc_low, w_bc) + over_columns(dt_low, w_dt)
    norm_gain_part = jnp.sum(d_normed * x_float * inv_rms[:, None], axis=0)
    d_rows = lax.psum_scatter(
        d_normed.astype(jnp.bfloat16), "tensor", scatter_dimension=0, tiled=True
    ).astype(jnp.float32)
    rms_rows = lax.dynamic_slice_in_dim(inv_rms, first_row, share, 0)
    cot_rows = lax.dynamic_slice_in_dim(cotangent, first_row, share, 0).astype(jnp.float32)
    gained = d_rows * norm_gain
    spread = rms_rows * rms_rows * rms_rows * jnp.sum(gained * x_rows, axis=-1) / features
    d_input = cot_rows + rms_rows[:, None] * gained - x_rows * spread[:, None]
    input_grad = lax.all_gather(d_input.astype(jnp.bfloat16), "tensor", axis=0, tiled=True)
    w_zx_grad, w_dt_grad, w_out_grad = (
        lax.psum_scatter(
            w_zx_part.astype(jnp.bfloat16), "dp", scatter_dimension=0, tiled=True
        ).astype(jnp.float32),
        lax.psum_scatter(
            w_dt_part.astype(jnp.bfloat16), "dp", scatter_dimension=0, tiled=True
        ).astype(jnp.float32),
        lax.psum_scatter(
            w_out_part.astype(jnp.bfloat16), "dp", scatter_dimension=1, tiled=True
        ).astype(jnp.float32),
    )
    conv_x_grad, dt_bias_grad, a_log_grad, d_skip_grad, gate_gain_grad = lax.psum(
        (conv_x_part, dt_bias_part, a_log_part, d_skip_part, gate_gain_part), "dp"
    )
    norm_gain_grad, w_bc_grad, conv_bc_grad = lax.psum(
        (norm_gain_part, w_bc_part, conv_bc_part), ("dp", "tensor")
    )
    return (
        mixed,
        input_grad,
        norm_gain_grad,
        w_zx_grad,
        w_bc_grad,
        w_dt_grad,
        conv_x_grad,
        conv_bc_grad,
        dt_bias_grad,
        a_log_grad,
        d_skip_grad,
        gate_gain_grad,
        w_out_grad,
    )


def solution(mesh):
    return jax.shard_map(
        local,
        mesh=mesh,
        in_specs=(
            P("dp", None),
            P(),
            P(None, None, "tensor"),
            P(),
            P(None, "tensor"),
            P(None, "tensor"),
            P(),
            P("tensor"),
            P("tensor"),
            P("tensor"),
            P("tensor"),
            P("tensor", None),
            P("dp", None),
            P("dp"),
        ),
        out_specs=(
            P("dp", None),
            P("dp", None),
            P(),
            P("dp", None, "tensor"),
            P(),
            P("dp", "tensor"),
            P(None, "tensor"),
            P(),
            P("tensor"),
            P("tensor"),
            P("tensor"),
            P("tensor"),
            P("tensor", "dp"),
        ),
        check_vma=False,
    )
```

profile of v0, /device:TPU:0, one launch (start us, length us, event | category | flops | bytes accessed | tf_op | source)
XLA Modules:
  0.0 1176.5 jit_solution(15319442505596880165)
XLA Ops:
  12.6 32.8 %fusion.165 = (bf16[2048,1,2048]{2,1,0:T(2,128)(2,1)}, bf16[2048,1,2048]{2,1,0:T(2,128)(2,1)}) fusion(bf16[2048,2,2048]{2,1,0:T(2,128)(2,1)} %param.20), kind=kLoop, calls=%fused_computation.254 | loop fusion | bytes 33554432 | tf_op jit(solution)/shard_map/slice | solution.py:121
  46.5 13.6 %fusion.40 = f32[8,128,2048]{2,1,0:T(8,128)S(1)} fusion(bf16[8,128,2048]{2,1,0:T(8,128)(2,1)S(1)} %bitcast.263, bf16[2048,1,2048]{2,1,0:T(2,128)(2,1)} %get-tuple-element.380), kind=kOutput, calls=%fused_computation.63 | convolution fusion | flops 8589934592 | bytes 20971520 | tf_op jit(solution)/shard_map/dot_general | solution.py:122
  64.3 16.3 %multiply_convert_fusion.1 = (bf16[8,128,2048]{2,1,0:T(8,128)(2,1)}, f32[8,128,2048]{2,1,0:T(8,128)}) fusion(f32[8,128,2048]{2,1,0:T(8,128)} %copy-done.7, f32[2048]{0:T(1024)S(1)} %bitcast.305, f32[8,3,2048]{2,1,0:T(4,128)S(1)} %select_select_fusion, f32[2048]{0:T(1024)S(1)} %bitcast.307, f32[2048]{0:T(1024)S(1)} %bitcast.301, f32[2048]{0:T(1024)S(1)} %bitcast.303, ...), kind=kLoop, calls=%fused_computation.101 | loop fusion | flops 33554432 | bytes 21209088 | tf_op jit(solution)/shard_map/convert_element_type | solution.py:94
  80.6 13.3 %reshape.279 = f32[8,128,32,64]{3,2,1,0:T(8,128)} reshape(bf16[1024,2048]{1,0:T(8,128)(2,1)} %bitcast.260) | data formatting | bytes 12582912 | tf_op jit(solution)/shard_map/jvp()/reshape;jvp()/reshape | solution.py:49
  104.8 23.3 %fusion.171 = f32[8,128,32]{2,0,1:T(8,128)S(1)} fusion(f32[8,128,32]{2,0,1:T(8,128)S(1)} %copy.143), kind=kOutput, calls=%fused_computation.260 | output fusion | flops 4161536 | bytes 262144 | tf_op jit(solution)/shard_map/jvp(jit(cumsum))/reduce_window_sum | solution.py:53
  130.3 14.9 %copy.158 = f32[8,128,32,64]{1,3,2,0:T(8,128)} copy(f32[8,128,32,64]{3,2,1,0:T(8,128)} %reshape.279) | data formatting | bytes 16777216 | tf_op jit(solution)/shard_map/jvp()/reshape;jvp()/reshape | solution.py:49
  161.8 9.1 while.30
  170.9 7.6 fusion.48
  178.5 13.6 %fusion.73 = f32[32,64,128,8]{2,3,1,0:T(8,128)S(1)} fusion(f32[8,32,64,128]{3,2,1,0:T(8,128)S(1)} %fusion.48, f32[32,8,8]{2,1,0:T(8,128)S(1)} %get-tuple-element.163), kind=kOutput, calls=%fused_computation.120 | convolution fusion | flops 201326592 | bytes 16785408 | tf_op jit(solution)/shard_map/jvp(hba,ahpn->bhpn)/dot_general | solution.py:64
  198.5 9.5 fusion.69
  211.3 21.9 %fusion.39 = f32[8,128,32,64]{1,3,2,0:T(8,128)} fusion(f32[8,128,32,64]{1,3,2,0:T(8,128)} %copy.158, f32[8,128,32,64]{1,3,2,0:T(8,128)S(1)} %fusion.69, f32[32]{0:T(128)S(1)} %copy-done.90, f32[8,128,32]{1,2,0:T(8,128)S(1)} %copy.148, f32[8,128,32]{1,2,0:T(8,128)S(1)} %bitcast.298, f32[8,128,32]{1,2,0:T(8,128)S(1)} %copy-done.36, ...), kind=kOutput, calls=%fused_computation.62 | convolution fusion | flops 3250585600 | bytes 30294144 | tf_op jit(solution)/shard_map/jvp(bijh,bjhp->bihp)/dot_general | solution.py:60
  233.2 16.2 %copy.215 = f32[8,128,32,64]{3,2,1,0:T(8,128)} copy(f32[8,128,32,64]{1,3,2,0:T(8,128)} %fusion.39) | data formatting | bytes 16777216 | tf_op jit(solution)/shard_map/jvp()/reshape | solution.py:70
  249.4 14.8 %reshape.284 = f32[1024,2048]{1,0:T(8,128)} reshape(f32[8,128,32,64]{3,2,1,0:T(8,128)} %copy.215) | data formatting | bytes 16777216 | tf_op jit(solution)/shard_map/jvp()/reshape | solution.py:70
  264.3 19.7 %multiply_reduce_fusion.11 = (f32[1024]{0:T(1024)S(1)}, f32[1024,2048]{1,0:T(8,128)}, f32[1024,2048]{1,0:T(8,128)}) fusion(f32[1024,2048]{1,0:T(8,128)} %reshape.284, bf16[1024,2048]{1,0:T(8,128)(2,1)} %copy-done.2, bf16[2048,1,2048]{2,1,0:T(2,128)(2,1)} %get-tuple-element.379), kind=kOutput, calls=%fused_computation.85 | convolution fusion | flops 8604613632 | bytes 37752832 | tf_op jit(solution)/shard_map/dot_general | solution.py:121
  289.9 15.3 %convolution_convert_fusion.1 = bf16[1024,2048]{1,0:T(8,128)(2,1)} fusion(bf16[2048,2048]{1,0:T(8,128)(2,1)} %param.29, f32[1024,2048]{1,0:T(8,128)} %get-tuple-element.373, f32[2048]{0:T(1024)S(1)} %copy-done.73, f32[1024]{0:T(1024)S(1)} %add_rsqrt_fusion), kind=kOutput, calls=%fused_computation.140 | convolution fusion | flops 8598323200 | bytes 20983808 | tf_op jit(solution)/shard_map/dot_general | solution.py:150
  305.2 17.0 %multiply_reduce_fusion.2 = (f32[2048]{0:T(1024)}, f32[1024]{0:T(1024)S(1)}, f32[1024,2048]{1,0:T(8,128)}) fusion(f32[1024,2048]{1,0:T(8,128)} %get-tuple-element.373, f32[1024]{0:T(1024)S(1)} %add_rsqrt_fusion, f32[2048]{0:T(1024)S(1)} %copy-done.73, bf16[1024,2048]{1,0:T(8,128)(2,1)} %param.30, bf16[2048,2048]{1,0:T(8,128)(2,1)} %param.29), kind=kOutput, calls=%fused_computation.70 | convolution fusion | flops 8602514432 | bytes 29384704 | tf_op jit(solution)/shard_map/dot_general | solution.py:88
  327.2 20.5 %multiply_reduce_fusion.3 = (f32[2048]{0:T(1024)}, f32[1024,2048]{1,0:T(8,128)}, bf16[1024,2048]{1,0:T(8,128)(2,1)}) fusion(bf16[1024,2048]{1,0:T(8,128)(2,1)} %bitcast.262, f32[1024,2048]{1,0:T(8,128)} %get-tuple-element.413, f32[1024,2048]{1,0:T(8,128)} %get-tuple-element.373, f32[1024]{0:T(1024)S(1)} %fusion.141, f32[1024,2048]{1,0:T(8,128)} %get-tuple-element.414, ...), kind=kLoop, calls=%fused_computation.71 | loop fusion | flops 41940992 | bytes 50356224 | tf_op jit(solution)/shard_map/transpose(jvp())/reduce_sum | solution.py:69
  347.7 9.3 copy.163
  362.4 6.6 fusion.76
  369.1 12.3 %fusion.44 = f32[32,64,128,8]{2,3,1,0:T(8,128)S(1)} fusion(f32[8,32,64,128]{3,2,1,0:T(8,128)} %fusion.76, s32[8]{0:T(128)S(1)} %copy-done.51), kind=kOutput, calls=%fused_computation.68 | convolution fusion | flops 201326656 | bytes 16777248 | tf_op jit(solution)/shard_map/transpose(jvp(bq,qhpn->bhpn))/dot_general | solution.py:65
  381.4 9.7 convolution_bitcast_fusion.1
  391.1 21.3 %fusion.106 = f32[32,8,8]{2,1,0:T(8,128)S(1)} fusion(f32[32,64,128,8]{2,3,1,0:T(8,128)S(1)} %fusion.44, f32[8,32,64,128]{3,2,1,0:T(8,128)S(1)} %bitcast.259), kind=kOutput, calls=%fused_computation.159 | convolution fusion | flops 201326592 | bytes 16785408 | tf_op jit(solution)/shard_map/transpose(jvp(hba,ahpn->bhpn))/dot_general | solution.py:64
  412.5 6.8 multiply_reduce_fusion.9
  419.3 10.4 fusion.65
  429.7 18.2 %fusion.103 = f32[8,128,128]{2,1,0:T(8,128)S(1)} fusion(f32[8,32,64,128]{3,0,2,1:T(8,128)} %convolution_bitcast_fusion.1, f32[8,128,32]{1,2,0:T(8,128)S(1)} %copy-done.29, bf16[8,128,32,64]{1,0,3,2:T(8,128)(2,1)S(1)} %bitcast.266), kind=kOutput, calls=%fused_computation.156 | convolution fusion | flops 3225419776 | bytes 13238272 | tf_op jit(solution)/shard_map/transpose(jvp(bjh,bjhp,bjn->bhpn))/dot_general | solution.py:62
  448.0 15.7 %fusion.98 = f32[8,128,128]{2,1,0:T(8,128)S(1)} fusion(f32[8,32,64,128]{3,0,2,1:T(8,128)S(1)} %bitcast.257, f32[8,128,32,64]{1,0,3,2:T(8,128)S(1)} %bitcast.252, f32[8,128,32]{1,2,0:T(8,128)S(1)} %copy.148), kind=kOutput, calls=%fused_computation.155 | convolution fusion | flops 3223322624 | bytes 17432576 | tf_op jit(solution)/shard_map/transpose(jvp(bin,bhpn->bihp))/dot_general | solution.py:66
  463.8 28.9 %fusion.28 = (f32[8,128,32]{1,2,0:T(8,128)}, f32[8,128,32]{1,2,0:T(8,128)S(1)}, f32[8,128,32]{1,2,0:T(8,128)}, f32[8,128,128]{2,1,0:T(8,128)S(1)}) fusion(f32[8,128,32]{1,2,0:T(8,128)S(1)} %bitcast.299, f32[8,128,32]{1,2,0:T(8,128)S(1)} %copy-done.37, f32[8,128,128]{2,1,0:T(8,128)S(1)} %copy-done.31, pred[128,128]{1,0:T(8,128)(4,1)S(1)} %copy-done.64, ...), kind=kOutput, calls=%fused_computation.44 | convolution fusion | flops 3283910656 | bytes 14303232 | tf_op jit(solution)/shard_map/transpose(jvp(bijh,bjhp->bihp))/dot_general | solution.py:60
  497.8 10.7 multiply_reduce_fusion.1
  508.4 23.6 %bitcast_add_fusion = f32[8,128,32,64]{1,3,2,0:T(8,128)} fusion(f32[8,128,32,64]{1,3,2,0:T(8,128)} %fusion.65, f32[8,128,32,64]{1,0,3,2:T(8,128)S(1)} %bitcast.255, f32[32]{0:T(128)S(1)} %copy-done.91, f32[8,128,32]{1,2,0:T(8,128)S(1)} %copy-done.29, f32[8,128,32]{1,2,0:T(8,128)S(1)} %bitcast.300, f32[8,128,32]{1,2,0:T(8,128)S(1)} %copy-done.37, ...), kind=kOutput, calls=%fused_computation.58 | convolution fusion | flops 3250585600 | bytes 34488448 | tf_op jit(solution)/shard_map/transpose(jvp(bijh,bjhp->bihp))/dot_general | solution.py:60
  536.4 36.3 %while.31 = (s32[]{:T(128)}, f32[8,32]{1,0:T(8,128)}, f32[32,8,8]{2,1,0:T(8,128)S(1)}, f32[8,32,8,8]{3,2,1,0:T(8,128)}, s32[8]{0:T(128)}, /*index=5*/f32[8,32]{0...) while((s32[]{:T(128)}, f32[8,32]{1,0:T(8,128)}, f32[32,8,8]{2,1,0:T(8,128)S(1)}, ...), condition=%wide.region_15.16_spmd.clone, body=%wide.region_14.15_spmd.clone.sunk | while | flops 420484 | bytes 210855 | solution.py:39
  581.3 9.2 copy.170
  590.6 18.6 %multiply_reduce_fusion.6 = (f32[2048]{0:T(1024)}, f32[2048]{0:T(1024)}, f32[2048]{0:T(1024)}, f32[2048]{0:T(1024)}, f32[2048]{0:T(1024)}, /*index=5*/f32[8,128,2048]{2,1,0:T(8,128)S(1)}) fusion(f32[8,128,2048]{2,1,0:T(8,128)} %copy-done.7, f32[8,3,2048]{2,1,0:T(4,128)S(1)} %copy-done.19, f32[8,128,2048]{2,1,0:T(8,128)} %get-tuple-element.377, ...), kind=kLoop, calls=%fused_computation.74 | loop fusion | flops 44029952 | bytes 33792000 | tf_op jit(solution)/shard_map/transpose(jvp())/reduce_sum | solution.py:22
  609.2 11.9 %broadcast_multiply_fusion = (f32[8,128,2048]{2,1,0:T(8,128)}, f32[8,128,2048]{2,1,0:T(8,128)}, f32[8,128,2048]{2,1,0:T(8,128)}, f32[8,128,2048]{2,1,0:T(8,128)}) fusion(f32[8,128,2048]{2,1,0:T(8,128)S(1)} %get-tuple-element.366, f32[2048]{0:T(1024)S(1)} %bitcast.306, f32[2048]{0:T(1024)S(1)} %bitcast.304, f32[2048]{0:T(1024)S(1)} %bitcast.302, ...), kind=kLoop, calls=%fused_computation.136 | loop fusion | flops 8388608 | bytes 41975808 | tf_op jit(solution)/shard_map/transpose(jvp())/mul | solution.py:22
  629.6 13.1 %pad_add_fusion = f32[8,131,2048]{2,1,0:T(8,128)S(1)} fusion(f32[8,128,2048]{2,1,0:T(8,128)} %get-tuple-element.384, f32[8,128,2048]{2,1,0:T(8,128)} %get-tuple-element.385, f32[8,128,2048]{2,1,0:T(8,128)} %get-tuple-element.386, f32[8,128,2048]{2,1,0:T(8,128)} %get-tuple-element.383), kind=kLoop, calls=%fused_computation.42 | loop fusion | flops 6438912 | bytes 42139648 | tf_op jit(solution)/shard_map/transpose(jvp())/add_any | solution.py:22
  650.6 15.6 %fusion.87 = f32[1024,2048]{1,0:T(8,128)} fusion(bf16[1024,2048]{1,0:T(8,128)(2,1)S(1)} %copy-done.15, bf16[2048,1,2048]{2,1,0:T(2,128)(2,1)} %get-tuple-element.379), kind=kOutput, calls=%fused_computation.142 | convolution fusion | flops 8589934592 | bytes 20971520 | tf_op jit(solution)/shard_map/dot_general | solution.py:88
  666.2 24.1 %multiply_reduce_fusion.8 = (f32[2048]{0:T(1024)S(1)}, bf16[1024,2048]{1,0:T(8,128)(2,1)}, bf16[1024,2048]{1,0:T(8,128)(2,1)}) fusion(bf16[1024,2048]{1,0:T(8,128)(2,1)} %param.18, f32[1024]{0:T(1024)S(1)} %copy-done.59, bf16[1024,2048]{1,0:T(8,128)(2,1)} %all-reduce.29.cloned.1.call-done, f32[1024,2048]{1,0:T(8,128)} %fusion.138, ...), kind=kOutput, calls=%fused_computation.78 | convolution fusion | flops 8613001216 | bytes 54538240 | tf_op jit(solution)/shard_map/dot_general | solution.py:88
  694.5 15.3 %convolution_convert_fusion = bf16[2048,2048]{1,0:T(8,128)(2,1)} fusion(bf16[1024,2048]{1,0:T(8,128)(2,1)} %param.30, f32[1024,2048]{1,0:T(8,128)} %get-tuple-element.373, f32[2048]{0:T(1024)S(1)} %copy-done.74, f32[1024]{0:T(1024)S(1)} %copy-done.62), kind=kOutput, calls=%fused_computation.125 | convolution fusion | flops 8600420352 | bytes 20983808 | tf_op jit(solution)/shard_map/dot_general | solution.py:82
  709.7 12.4 %copy.213 = bf16[2048,2048]{0,1:T(8,128)(2,1)} copy(bf16[2048,2048]{1,0:T(8,128)(2,1)} %convolution_convert_fusion) | data formatting | bytes 16777216
  722.2 6.6 convert_element_type.94
  728.9 17.5 %reduce-scatter.9.cloned.1.call-done = bf16[512,2048]{1,0:T(8,128)(2,1)} async-done(((bf16[1024,2048]{1,0:T(8,128)(2,1)}), bf16[512,2048]{1,0:T(8,128)(2,1)}) %reduce-scatter.9.cloned.1.call-update) | async-done | bytes 2097168 | tf_op jit(solution)/shard_map/reduce_scatter | solution.py:181
  755.9 12.7 %convert_bitcast_fusion.1 = bf16[2048,1,2048]{2,0,1:T(8,128)(2,1)S(1)} fusion(bf16[1024,2048]{1,0:T(8,128)(2,1)} %copy-done.2, bf16[1024,2048]{1,0:T(8,128)(2,1)} %bitcast.285), kind=kOutput, calls=%fused_computation.76 | convolution fusion | flops 8594128896 | bytes 16777216 | tf_op jit(solution)/shard_map/dot_general | solution.py:82
  768.6 9.8 convert_bitcast_fusion.2
  778.4 6.8 pad_maximum_fusion
  790.7 63.7 %all-reduce.25 = (f32[5,2048]{1,0:T(8,128)}, f32[32]{0:T(128)}, f32[32]{0:T(128)}, f32[32]{0:T(128)}, f32[2048]{0:T(1024)}) all-reduce(f32[5,2048]{1,0:T(8,128)S(1)} %pad_add_fusion.3, f32[32]{0:T(128)S(1)} %get-tuple-element.364, f32[32]{0:T(128)S(1)} %negate_multiply_fusion, ...), channel_id=1, replica_groups=mesh['dp'=16,'tensor'=2] {'dp'}, use_global_device_ids=true, to_apply=%region_32.33 | all-reduce | flops 12384 | bytes 99072 | tf_op jit(solution)/shard_map/psum | solution.py:201
  855.9 39.0 %all-reduce.24 = (f32[2048]{0:T(1024)}, f32[5,256]{1,0:T(8,128)}) all-reduce(f32[2048]{0:T(1024)S(1)} %get-tuple-element.381, f32[5,256]{1,0:T(8,128)S(1)} %pad_add_fusion.4), channel_id=1, replica_groups=mesh['dp'=16,'tensor'=2] {'dp','tensor'}, use_global_device_ids=true, to_apply=%region_23.24 | all-reduce | flops 3328 | bytes 26624 | tf_op jit(solution)/shard_map/psum | solution.py:204
  894.8 22.0 %reduce-scatter.15.cloned.1.call-done = bf16[128,2048]{1,0:T(8,128)(2,1)} async-done(((bf16[2048,2048]{1,0:T(8,128)(2,1)}), bf16[128,2048]{1,0:T(8,128)(2,1)}) %reduce-scatter.15.cloned.1.call-update) | async-done | bytes 524304
  919.2 56.4 %all-gather.2.cloned.1.call-done = bf16[1024,2048]{1,0:T(8,128)(2,1)} async-done(((bf16[512,2048]{1,0:T(8,128)(2,1)}), bf16[1024,2048]{1,0:T(8,128)(2,1)}) %all-gather.2.cloned.1.call-update) | async-done | bytes 4194320 | tf_op jit(solution)/shard_map/all_gather | solution.py:189
  975.6 183.1 %reduce-scatter.11.cloned.1.call-done = bf16[128,2,2048]{2,0,1:T(8,128)(2,1)} async-done(((bf16[2048,2,2048]{2,0,1:T(8,128)(2,1)}), bf16[128,2,2048]{2,0,1:T(8,128)(2,1)}) %reduce-scatter.11.cloned.1.call-update) | async-done | bytes 1048592 | tf_op jit(solution)/shard_map/reduce_scatter | solution.py:191
  (395 shorter events, 176.5 us)
Async XLA Ops:
  8.0 137.2 %copy-start = (bf16[2048,256]{1,0:T(8,128)(2,1)S(1)}, bf16[2048,256]{1,0:T(8,128)(2,1)}, u32[]{:S(2)}) copy-start(bf16[2048,256]{1,0:T(8,128)(2,1)} %param.21) | copy-start | bytes 3145732
  8.0 658.2 %all-reduce.29.cloned.1.call-start = ((), (), s32[]{:S(2)}) async-start(), calls=%async_computation.4 | async-start | bytes 8388608 | tf_op jit(solution)/shard_map/psum | solution.py:155
  8.8 51.4 %copy-start.79 = (s32[8]{0:T(128)}, s32[8]{0:T(128)S(1)}, u32[]{:S(2)}) copy-start(s32[8]{0:T(128)S(1)} %broadcast_maximum_fusion) | copy-start | bytes 100
  9.5 139.9 %copy-start.76 = (pred[8]{0:T(512)(128)(4,1)}, pred[8]{0:T(512)(128)(4,1)S(1)}, u32[]{:S(2)}) copy-start(pred[8]{0:T(512)(128)(4,1)S(1)} %get-tuple-element.411) | copy-start | bytes 28
  12.6 32.9 %copy-start.58 = (f32[1024]{0:T(1024)}, f32[1024]{0:T(1024)S(1)}, u32[]{:S(2)}) copy-start(f32[1024]{0:T(1024)S(1)} %add_rsqrt_fusion.1) | copy-start | bytes 12292
  12.6 32.8 %copy-start.60 = (f32[5,2048]{1,0:T(8,128)S(1)}, f32[5,2048]{1,0:T(8,128)}, u32[]{:S(2)}) copy-start(f32[5,2048]{1,0:T(8,128)} %param.23) | copy-start | bytes 122884
  12.6 32.9 %copy-start.6 = (bf16[1024,2048]{1,0:T(8,128)(2,1)S(1)}, bf16[1024,2048]{1,0:T(8,128)(2,1)}, u32[]{:S(2)}) copy-start(bf16[1024,2048]{1,0:T(8,128)(2,1)} %param.18) | copy-start | bytes 12582916
  12.6 32.9 %copy-start.48 = (f32[2048]{0:T(1024)S(1)}, f32[2048]{0:T(1024)}, u32[]{:S(2)}) copy-start(f32[2048]{0:T(1024)} %param.19) | copy-start | bytes 24580
  45.5 18.8 %copy-start.40 = (f32[1,2048]{1,0:T(1,128)}, f32[1,2048]{1,0:T(1,128)S(1)}, u32[]{:S(2)}) copy-start(f32[1,2048]{1,0:T(1,128)S(1)} %get-tuple-element.402) | copy-start | bytes 24580
  45.5 18.8 %copy-start.42 = (f32[1,2048]{1,0:T(1,128)}, f32[1,2048]{1,0:T(1,128)S(1)}, u32[]{:S(2)}) copy-start(f32[1,2048]{1,0:T(1,128)S(1)} %get-tuple-element.403) | copy-start | bytes 24580
  45.5 18.8 %copy-start.44 = (f32[1,2048]{1,0:T(1,128)}, f32[1,2048]{1,0:T(1,128)S(1)}, u32[]{:S(2)}) copy-start(f32[1,2048]{1,0:T(1,128)S(1)} %get-tuple-element.404) | copy-start | bytes 24580
  45.5 18.8 %copy-start.46 = (f32[1,2048]{1,0:T(1,128)}, f32[1,2048]{1,0:T(1,128)S(1)}, u32[]{:S(2)}) copy-start(f32[1,2048]{1,0:T(1,128)S(1)} %get-tuple-element.405) | copy-start | bytes 24580
  93.9 35.0 %copy-start.51 = (s32[8]{0:T(128)S(1)}, s32[8]{0:T(128)}, u32[]{:S(2)}) copy-start(s32[8]{0:T(128)} %param.31) | copy-start | bytes 100
  100.4 29.3 %copy-start.88 = (f32[32]{0:T(128)}, f32[32]{0:T(128)S(1)}, u32[]{:S(2)}) copy-start(f32[32]{0:T(128)S(1)} %exponential_negate_fusion) | copy-start | bytes 388
  128.1 24.1 %copy-start.9 = (f32[8,128,32]{2,0,1:T(8,128)}, f32[8,128,32]{2,0,1:T(8,128)S(1)}, u32[]{:S(2)}) copy-start(f32[8,128,32]{2,0,1:T(8,128)S(1)} %fusion.171) | copy-start | bytes 393220
  128.2 24.1 %copy-start.50 = (f32[8,32]{1,0:T(8,128)}, f32[8,32]{1,0:T(8,128)S(1)}, u32[]{:S(2)}) copy-start(f32[8,32]{1,0:T(8,128)S(1)} %slice_bitcast_fusion) | copy-start | bytes 3076
  128.8 32.9 %copy-start.34 = (f32[8,8]{0,1:T(8,128)}, f32[8,8]{0,1:T(8,128)S(1)}, u32[]{:S(2)}) copy-start(f32[8,8]{0,1:T(8,128)S(1)} %fusion.143) | copy-start | bytes 772
  130.3 18.4 %copy-start.86 = (f32[5,256]{1,0:T(8,128)S(1)}, f32[5,256]{1,0:T(8,128)}, u32[]{:S(2)}) copy-start(f32[5,256]{1,0:T(8,128)} %param.24) | copy-start | bytes 15364
  155.6 22.9 %copy-start.28 = (f32[8,128,32]{1,2,0:T(8,128)}, f32[8,128,32]{1,2,0:T(8,128)S(1)}, u32[]{:S(2)}) copy-start(f32[8,128,32]{1,2,0:T(8,128)S(1)} %copy.150) | copy-start | bytes 393220
  170.9 21.2 %copy-start.22 = (f32[8,32]{0,1:T(8,128)}, f32[8,32]{0,1:T(8,128)S(1)}, u32[]{:S(2)}) copy-start(f32[8,32]{0,1:T(8,128)S(1)} %get-tuple-element.591) | copy-start | bytes 3076
  208.3 24.9 %copy-start.30 = (f32[8,128,128]{2,1,0:T(8,128)}, f32[8,128,128]{2,1,0:T(8,128)S(1)}, u32[]{:S(2)}) copy-start(f32[8,128,128]{2,1,0:T(8,128)S(1)} %fusion.173) | copy-start | bytes 1572868
  264.3 25.6 %copy-start.73 = (f32[2048]{0:T(1024)S(1)}, f32[2048]{0:T(1024)}, u32[]{:S(2)}) copy-start(f32[2048]{0:T(1024)} %param.28) | copy-start | bytes 24580
  289.8 37.3 %copy-start.61 = (f32[1024]{0:T(1024)}, f32[1024]{0:T(1024)S(1)}, u32[]{:S(2)}) copy-start(f32[1024]{0:T(1024)S(1)} %add_rsqrt_fusion) | copy-start | bytes 12292
  305.2 441.2 %reduce-scatter.9.cloned.1.call-start = ((), (), s32[]{:S(2)}) async-start(), calls=%async_computation.5 | async-start | bytes 6291456 | tf_op jit(solution)/shard_map/reduce_scatter | solution.py:181
  369.1 22.0 %slice-start.2 = ((s8[8388608]{0:T(1024)(128)(4,1)}), s8[4194304]{0:T(1024)(128)(4,1)S(1)}, s32[]{:S(2)}) async-start(s8[8388608]{0:T(1024)(128)(4,1)} %bitcast.258), calls=%async_computation.13 | async-start | bytes 8388608
  419.3 28.6 %slice-start = ((s8[8388608]{0:T(1024)(128)(4,1)}), s8[4194304]{0:T(1024)(128)(4,1)S(1)}, s32[]{:S(2)}) async-start(s8[8388608]{0:T(1024)(128)(4,1)} %bitcast.256), calls=%async_computation.11 | async-start | bytes 8388608
  429.7 18.2 %slice-start.1 = ((s8[8388608]{0:T(1024)(128)(4,1)}), s8[4194304]{0:T(1024)(128)(4,1)S(1)}, s32[]{:S(2)}) async-start(s8[8388608]{0:T(1024)(128)(4,1)} %bitcast.256), calls=%async_computation.12 | async-start | bytes 8388608
  463.7 30.0 %copy-start.12 = (f32[1024,256]{1,0:T(8,128)S(1)}, f32[1024,256]{1,0:T(8,128)}, u32[]{:S(2)}) copy-start(f32[1024,256]{1,0:T(8,128)} %copy-done.11) | copy-start | bytes 3145732
  463.7 30.0 %copy-start.17 = (f32[8,128,256]{2,1,0:T(8,128)S(1)}, f32[8,128,256]{2,1,0:T(8,128)}, u32[]{:S(2)}) copy-start(f32[8,128,256]{2,1,0:T(8,128)} %get-tuple-element.375) | copy-start | bytes 3145732
  463.7 30.0 %copy-start.33 = (f32[8,3,256]{2,1,0:T(4,128)S(1)}, f32[8,3,256]{2,1,0:T(4,128)}, u32[]{:S(2)}) copy-start(f32[8,3,256]{2,1,0:T(4,128)} %copy-done.32) | copy-start | bytes 73732
  508.4 28.0 %copy-start.23 = (f32[8,32]{0,1:T(8,128)S(1)}, f32[8,32]{0,1:T(8,128)}, u32[]{:S(2)}) copy-start(f32[8,32]{0,1:T(8,128)} %copy-done.22) | copy-start | bytes 3076
  532.1 40.7 %copy-start.10 = (f32[8,128,32]{2,0,1:T(8,128)S(1)}, f32[8,128,32]{2,0,1:T(8,128)}, u32[]{:S(2)}) copy-start(f32[8,128,32]{2,0,1:T(8,128)} %copy-done.9) | copy-start | bytes 393220
  532.1 43.3 %copy-start.13 = (f32[8,128,32]{2,0,1:T(8,128)S(1)}, f32[8,128,32]{2,0,1:T(8,128)}, u32[]{:S(2)}) copy-start(f32[8,128,32]{2,0,1:T(8,128)} %copy.149) | copy-start | bytes 393220
  590.5 18.6 %copy-start.41 = (f32[1,2048]{1,0:T(1,128)S(1)}, f32[1,2048]{1,0:T(1,128)}, u32[]{:S(2)}) copy-start(f32[1,2048]{1,0:T(1,128)} %copy-done.40) | copy-start | bytes 24580
  590.5 18.6 %copy-start.43 = (f32[1,2048]{1,0:T(1,128)S(1)}, f32[1,2048]{1,0:T(1,128)}, u32[]{:S(2)}) copy-start(f32[1,2048]{1,0:T(1,128)} %copy-done.42) | copy-start | bytes 24580
  590.5 18.6 %copy-start.45 = (f32[1,2048]{1,0:T(1,128)S(1)}, f32[1,2048]{1,0:T(1,128)}, u32[]{:S(2)}) copy-start(f32[1,2048]{1,0:T(1,128)} %copy-done.44) | copy-start | bytes 24580
  590.5 18.6 %copy-start.47 = (f32[1,2048]{1,0:T(1,128)S(1)}, f32[1,2048]{1,0:T(1,128)}, u32[]{:S(2)}) copy-start(f32[1,2048]{1,0:T(1,128)} %copy-done.46) | copy-start | bytes 24580
  690.3 164.1 %reduce-scatter.13.cloned.1.call-start = ((), (), s32[]{:S(2)}) async-start(), calls=%async_computation.9 | async-start | bytes 557056
  694.4 222.4 %reduce-scatter.15.cloned.1.call-start = ((), (), s32[]{:S(2)}) async-start(), calls=%async_computation.10 | async-start | bytes 8912896
  722.2 24.2 %copy-start.49 = (f32[2048]{0:T(1024)S(1)}, f32[2048]{0:T(1024)}, u32[]{:S(2)}) copy-start(f32[2048]{0:T(1024)} %param.19) | copy-start | bytes 24580
  722.2 253.4 %all-gather.2.cloned.1.call-start = ((), (), s32[]{:S(2)}) async-start(), calls=%async_computation.6 | async-start | bytes 6291456 | tf_op jit(solution)/shard_map/all_gather | solution.py:189
  755.8 402.9 %reduce-scatter.11.cloned.1.call-start = ((), (), s32[]{:S(2)}) async-start(), calls=%async_computation.7 | async-start | bytes 17825792 | tf_op jit(solution)/shard_map/reduce_scatter | solution.py:191
  785.4 69.0 %copy-start.81 = (f32[256]{0:T(256)S(1)}, f32[256]{0:T(256)}, u32[]{:S(2)}) copy-start(f32[256]{0:T(256)} %get-tuple-element.326) | copy-start | bytes 3076
  785.4 69.0 %copy-start.82 = (f32[256]{0:T(256)S(1)}, f32[256]{0:T(256)}, u32[]{:S(2)}) copy-start(f32[256]{0:T(256)} %get-tuple-element.327) | copy-start | bytes 3076
  785.4 69.0 %copy-start.83 = (f32[256]{0:T(256)S(1)}, f32[256]{0:T(256)}, u32[]{:S(2)}) copy-start(f32[256]{0:T(256)} %get-tuple-element.328) | copy-start | bytes 3076
  785.4 69.0 %copy-start.84 = (f32[256]{0:T(256)S(1)}, f32[256]{0:T(256)}, u32[]{:S(2)}) copy-start(f32[256]{0:T(256)} %get-tuple-element.329) | copy-start | bytes 3076
  785.4 69.0 %copy-start.85 = (f32[256]{0:T(256)S(1)}, f32[256]{0:T(256)}, u32[]{:S(2)}) copy-start(f32[256]{0:T(256)} %get-tuple-element.330) | copy-start | bytes 3076
  785.4 376.9 %all-reduce.31.cloned.1.call-start = ((), (), s32[]{:S(2)}) async-start(), calls=%async_computation.8 | async-start | bytes 4194304 | tf_op jit(solution)/shard_map/psum | solution.py:204
  (57 other events, 447.8 us)
Sparse Core Ops, SparseCore 0:
  305.3 109.7 all-reduce.28
  690.4 55.9 reduce-scatter.8
  750.5 56.5 reduce-scatter.12
  811.6 105.2 reduce-scatter.14
  918.9 56.6 all-gather.1
  980.1 178.5 reduce-scatter.10
Sparse Core Ops, SparseCore 1:
  792.7 204.7 all-reduce.30
where the time goes:
time: 1190 us; the launch traced here: 1180 us
  matrix products  397 us (33%)
  waiting for transfers between devices  279 us (23%)
  other arithmetic  188 us (16%)
  local copies, waits for them, and re-layouts  181 us (15%)
  blocking collectives  113 us (9%)
  between operations  17.5 us (1%)
    reduce_scatter x1, waiting for transfers between devices, local(): lax.psum_scatter(w_zx_part.astype(jnp.bfloat16), 'dp', scatter_dimension=...  183 us
    dot_general x3, matrix products, ssd_mix(): within = jnp.einsum('bijh,bjhp->bihp', weights, x_blocks, precision=highest)  74.5 us
    dot_general x5, matrix products, over_columns(): lax.dot_general(left, right, (((1,), (1,)), ((), ())), preferred_element_...  65.7 us
    psum x1, blocking collectives, local(): lax.psum((conv_x_part, dt_bias_part, a_log_part, d_skip_part, gate_gain_p...  63.7 us
    all_gather x1, waiting for transfers between devices, local(): lax.all_gather(d_input.astype(jnp.bfloat16), 'tensor', axis=0, tiled=True)  56.4 us
    dot_general x5, matrix products, over_tokens(): lax.dot_general(left, right, (((0,), (0,)), ((), ())), preferred_element_...  45.6 us
    dot_general x3, matrix products, ssd_mix(): jnp.einsum('hba,ahpn->bhpn', paths, local_states, precision=highest)  44.6 us
    unnamed x209, local copies, waits for them, and re-layouts  44.2 us
  transfers between devices with their start and end apart: 7, of which 4 were waited for; matrix products, arithmetic and copies ran while one was open for 38% of the time, Pallas kernels for 0%

commit v1 on v0

--- a/solution.py
+++ b/solution.py
@@ -1,3 +1,4 @@
+import functools
 import jax
 import jax.numpy as jnp
 from jax import lax
@@ -5,6 +6,14 @@
 
 epsilon = 1e-05
 highest = lax.Precision.HIGHEST
+
+
+def test_heads(incoming_x, axis_tag, mesh_ax):
+    y2 = jax.lax.psum(jax.lax.psum(incoming_x, axis_tag), mesh_ax)
+    return y2
+
+
+manage_skins_all = functools.partial(test_heads, axis_tag="tensor", mesh_ax="dp")
 
 
 def conv_path(inputs, kernel, parent):
@@ -201,8 +210,8 @@
     conv_x_grad, dt_bias_grad, a_log_grad, d_skip_grad, gate_gain_grad = lax.psum(
         (conv_x_part, dt_bias_part, a_log_part, d_skip_part, gate_gain_part), "dp"
     )
-    norm_gain_grad, w_bc_grad, conv_bc_grad = lax.psum(
-        (norm_gain_part, w_bc_part, conv_bc_part), ("dp", "tensor")
+    norm_gain_grad, w_bc_grad, conv_bc_grad = manage_skins_all(
+        (norm_gain_part, w_bc_part, conv_bc_part)
     )
     return (
         mixed,

time: 1190 us -> 1350 us (1.13)
  waiting for transfers between devices: 279 us -> 471 us
  blocking collectives: 113 us -> 81.1 us
    psum x1 -> x2, waiting for transfers between devices: 0.01 us -> 124 us  [test_heads(): y2 = jax.lax.psum(jax.lax.psum(incoming_x, axis_tag), mesh_ax)]
    unnamed x9 -> x10, waiting for transfers between devices: 22.1 us -> 96.3 us
    psum x2, blocking collectives: 103 us -> 70.3 us  [test_heads(): y2 = jax.lax.psum(jax.lax.psum(incoming_x, axis_tag), mesh_ax)]
  transfers between devices with their start and end apart: 7 -> 8, of which waited for: 4 -> 7; matrix products, arithmetic and copies ran while one was open for 38% -> 33% of each run, Pallas kernels for 0% -> 0%
where the time goes in v1:
time: 1350 us; the launch traced here: 1330 us
  waiting for transfers between devices  471 us (35%)
  matrix products  397 us (29%)
  other arithmetic  188 us (14%)
  local copies, waits for them, and re-layouts  181 us (13%)
  blocking collectives  81.1 us (6%)
  between operations  16.1 us (1%)
    reduce_scatter x1, waiting for transfers between devices, local(): lax.psum_scatter(w_zx_part.astype(jnp.bfloat16), 'dp', scatter_dimension=...  183 us
    psum x2, waiting for transfers between devices, test_heads(): y2 = jax.lax.psum(jax.lax.psum(incoming_x, axis_tag), mesh_ax)  124 us
    unnamed x10, waiting for transfers between devices  96.3 us
    dot_general x3, matrix products, ssd_mix(): within = jnp.einsum('bijh,bjhp->bihp', weights, x_blocks, precision=highest)  74.5 us
    psum x2, blocking collectives, test_heads(): y2 = jax.lax.psum(jax.lax.psum(incoming_x, axis_tag), mesh_ax)  70.3 us
    dot_general x5, matrix products, over_columns(): lax.dot_general(left, right, (((1,), (1,)), ((), ())), preferred_element_...  65.7 us
    all_gather x1, waiting for transfers between devices, local(): lax.all_gather(d_input.astype(jnp.bfloat16), 'tensor', axis=0, tiled=True)  56.2 us
    dot_general x5, matrix products, over_tokens(): lax.dot_general(left, right, (((0,), (0,)), ((), ())), preferred_element_...  45.5 us
  transfers between devices with their start and end apart: 8, of which 7 were waited for; matrix products, arithmetic and copies ran while one was open for 33% of the time, Pallas kernels for 0%

profile of v1, /device:TPU:0, one launch (start us, length us, event | category | flops | bytes accessed | tf_op | source)
XLA Modules:
  0.0 1334.9 jit_solution(10548173623647683377)
XLA Ops:
  11.8 32.8 %fusion.165 = (bf16[2048,1,2048]{2,1,0:T(2,128)(2,1)}, bf16[2048,1,2048]{2,1,0:T(2,128)(2,1)}) fusion(bf16[2048,2,2048]{2,1,0:T(2,128)(2,1)} %param.20), kind=kLoop, calls=%fused_computation.254 | loop fusion | bytes 33554432 | tf_op jit(solution)/shard_map/slice | solution.py:130
  45.7 13.6 %fusion.40 = f32[8,128,2048]{2,1,0:T(8,128)S(1)} fusion(bf16[8,128,2048]{2,1,0:T(8,128)(2,1)S(1)} %bitcast.263, bf16[2048,1,2048]{2,1,0:T(2,128)(2,1)} %get-tuple-element.382), kind=kOutput, calls=%fused_computation.63 | convolution fusion | flops 8589934592 | bytes 20971520 | tf_op jit(solution)/shard_map/dot_general | solution.py:131
  63.4 16.3 %multiply_convert_fusion.1 = (bf16[8,128,2048]{2,1,0:T(8,128)(2,1)}, f32[8,128,2048]{2,1,0:T(8,128)}) fusion(f32[8,128,2048]{2,1,0:T(8,128)} %copy-done.7, f32[2048]{0:T(1024)S(1)} %bitcast.305, f32[8,3,2048]{2,1,0:T(4,128)S(1)} %select_select_fusion, f32[2048]{0:T(1024)S(1)} %bitcast.307, f32[2048]{0:T(1024)S(1)} %bitcast.301, f32[2048]{0:T(1024)S(1)} %bitcast.303, ...), kind=kLoop, calls=%fused_computation.101 | loop fusion | flops 33554432 | bytes 21209088 | tf_op jit(solution)/shard_map/convert_element_type | solution.py:103
  79.8 13.3 reshape.279
  104.0 23.3 %fusion.171 = f32[8,128,32]{2,0,1:T(8,128)S(1)} fusion(f32[8,128,32]{2,0,1:T(8,128)S(1)} %copy.143), kind=kOutput, calls=%fused_computation.260 | output fusion | flops 4161536 | bytes 262144 | tf_op jit(solution)/shard_map/jvp(jit(cumsum))/reduce_window_sum | solution.py:62
  129.5 15.0 %copy.158 = f32[8,128,32,64]{1,3,2,0:T(8,128)} copy(f32[8,128,32,64]{3,2,1,0:T(8,128)} %reshape.279) | data formatting | bytes 16777216 | tf_op jit(solution)/shard_map/jvp()/reshape;jvp()/reshape | solution.py:58
  161.1 9.1 while.30
  170.2 7.6 fusion.48
  177.8 13.6 %fusion.73 = f32[32,64,128,8]{2,3,1,0:T(8,128)S(1)} fusion(f32[8,32,64,128]{3,2,1,0:T(8,128)S(1)} %fusion.48, f32[32,8,8]{2,1,0:T(8,128)S(1)} %get-tuple-element.163), kind=kOutput, calls=%fused_computation.120 | convolution fusion | flops 201326592 | bytes 16785408 | tf_op jit(solution)/shard_map/jvp(hba,ahpn->bhpn)/dot_general | solution.py:73
  197.7 9.5 fusion.69
  210.5 21.9 %fusion.39 = f32[8,128,32,64]{1,3,2,0:T(8,128)} fusion(f32[8,128,32,64]{1,3,2,0:T(8,128)} %copy.158, f32[8,128,32,64]{1,3,2,0:T(8,128)S(1)} %fusion.69, f32[32]{0:T(128)S(1)} %copy-done.90, f32[8,128,32]{1,2,0:T(8,128)S(1)} %copy.148, f32[8,128,32]{1,2,0:T(8,128)S(1)} %bitcast.298, f32[8,128,32]{1,2,0:T(8,128)S(1)} %copy-done.36, ...), kind=kOutput, calls=%fused_computation.62 | convolution fusion | flops 3250585600 | bytes 30294144 | tf_op jit(solution)/shard_map/jvp(bijh,bjhp->bihp)/dot_general | solution.py:69
  232.5 16.2 %copy.215 = f32[8,128,32,64]{3,2,1,0:T(8,128)} copy(f32[8,128,32,64]{1,3,2,0:T(8,128)} %fusion.39) | data formatting | bytes 16777216 | tf_op jit(solution)/shard_map/jvp()/reshape | solution.py:79
  248.7 14.8 %reshape.284 = f32[1024,2048]{1,0:T(8,128)} reshape(f32[8,128,32,64]{3,2,1,0:T(8,128)} %copy.215) | data formatting | bytes 16777216 | tf_op jit(solution)/shard_map/jvp()/reshape | solution.py:79
  263.5 19.7 %multiply_reduce_fusion.11 = (f32[1024]{0:T(1024)S(1)}, f32[1024,2048]{1,0:T(8,128)}, f32[1024,2048]{1,0:T(8,128)}) fusion(f32[1024,2048]{1,0:T(8,128)} %reshape.284, bf16[1024,2048]{1,0:T(8,128)(2,1)} %copy-done.2, bf16[2048,1,2048]{2,1,0:T(2,128)(2,1)} %get-tuple-element.381), kind=kOutput, calls=%fused_computation.85 | convolution fusion | flops 8604613632 | bytes 37752832 | tf_op jit(solution)/shard_map/dot_general | solution.py:130
  289.1 15.3 %convolution_convert_fusion.1 = bf16[1024,2048]{1,0:T(8,128)(2,1)} fusion(bf16[2048,2048]{1,0:T(8,128)(2,1)} %param.29, f32[1024,2048]{1,0:T(8,128)} %get-tuple-element.375, f32[2048]{0:T(1024)S(1)} %copy-done.73, f32[1024]{0:T(1024)S(1)} %add_rsqrt_fusion), kind=kOutput, calls=%fused_computation.140 | convolution fusion | flops 8598323200 | bytes 20983808 | tf_op jit(solution)/shard_map/dot_general | solution.py:159
  304.5 17.0 %multiply_reduce_fusion.2 = (f32[2048]{0:T(1024)}, f32[1024]{0:T(1024)S(1)}, f32[1024,2048]{1,0:T(8,128)}) fusion(f32[1024,2048]{1,0:T(8,128)} %get-tuple-element.375, f32[1024]{0:T(1024)S(1)} %add_rsqrt_fusion, f32[2048]{0:T(1024)S(1)} %copy-done.73, bf16[1024,2048]{1,0:T(8,128)(2,1)} %param.30, bf16[2048,2048]{1,0:T(8,128)(2,1)} %param.29), kind=kOutput, calls=%fused_computation.70 | convolution fusion | flops 8602514432 | bytes 29384704 | tf_op jit(solution)/shard_map/dot_general | solution.py:97
  326.4 20.5 %multiply_reduce_fusion.3 = (f32[2048]{0:T(1024)}, f32[1024,2048]{1,0:T(8,128)}, bf16[1024,2048]{1,0:T(8,128)(2,1)}) fusion(bf16[1024,2048]{1,0:T(8,128)(2,1)} %bitcast.262, f32[1024,2048]{1,0:T(8,128)} %get-tuple-element.415, f32[1024,2048]{1,0:T(8,128)} %get-tuple-element.375, f32[1024]{0:T(1024)S(1)} %fusion.141, f32[1024,2048]{1,0:T(8,128)} %get-tuple-element.416, ...), kind=kLoop, calls=%fused_computation.71 | loop fusion | flops 41940992 | bytes 50356224 | tf_op jit(solution)/shard_map/transpose(jvp())/reduce_sum | solution.py:78
  347.0 9.3 copy.163
  368.3 12.3 fusion.44
  380.6 9.7 convolution_bitcast_fusion.1
  390.4 21.3 %fusion.106 = f32[32,8,8]{2,1,0:T(8,128)S(1)} fusion(f32[32,64,128,8]{2,3,1,0:T(8,128)S(1)} %fusion.44, f32[8,32,64,128]{3,2,1,0:T(8,128)S(1)} %bitcast.259), kind=kOutput, calls=%fused_computation.159 | convolution fusion | flops 201326592 | bytes 16785408 | tf_op jit(solution)/shard_map/transpose(jvp(hba,ahpn->bhpn))/dot_general | solution.py:73
  418.5 10.4 fusion.65
  428.9 18.2 %fusion.103 = f32[8,128,128]{2,1,0:T(8,128)S(1)} fusion(f32[8,32,64,128]{3,0,2,1:T(8,128)} %convolution_bitcast_fusion.1, f32[8,128,32]{1,2,0:T(8,128)S(1)} %copy-done.29, bf16[8,128,32,64]{1,0,3,2:T(8,128)(2,1)S(1)} %bitcast.266), kind=kOutput, calls=%fused_computation.156 | convolution fusion | flops 3225419776 | bytes 13238272 | tf_op jit(solution)/shard_map/transpose(jvp(bjh,bjhp,bjn->bhpn))/dot_general | solution.py:71
  447.2 15.7 %fusion.98 = f32[8,128,128]{2,1,0:T(8,128)S(1)} fusion(f32[8,32,64,128]{3,0,2,1:T(8,128)S(1)} %bitcast.257, f32[8,128,32,64]{1,0,3,2:T(8,128)S(1)} %bitcast.252, f32[8,128,32]{1,2,0:T(8,128)S(1)} %copy.148), kind=kOutput, calls=%fused_computation.155 | convolution fusion | flops 3223322624 | bytes 17432576 | tf_op jit(solution)/shard_map/transpose(jvp(bin,bhpn->bihp))/dot_general | solution.py:75
  463.0 28.9 %fusion.28 = (f32[8,128,32]{1,2,0:T(8,128)}, f32[8,128,32]{1,2,0:T(8,128)S(1)}, f32[8,128,32]{1,2,0:T(8,128)}, f32[8,128,128]{2,1,0:T(8,128)S(1)}) fusion(f32[8,128,32]{1,2,0:T(8,128)S(1)} %bitcast.299, f32[8,128,32]{1,2,0:T(8,128)S(1)} %copy-done.37, f32[8,128,128]{2,1,0:T(8,128)S(1)} %copy-done.31, pred[128,128]{1,0:T(8,128)(4,1)S(1)} %copy-done.64, ...), kind=kOutput, calls=%fused_computation.44 | convolution fusion | flops 3283910656 | bytes 14303232 | tf_op jit(solution)/shard_map/transpose(jvp(bijh,bjhp->bihp))/dot_general | solution.py:69
  497.0 10.7 multiply_reduce_fusion.1
  507.7 23.6 %bitcast_add_fusion = f32[8,128,32,64]{1,3,2,0:T(8,128)} fusion(f32[8,128,32,64]{1,3,2,0:T(8,128)} %fusion.65, f32[8,128,32,64]{1,0,3,2:T(8,128)S(1)} %bitcast.255, f32[32]{0:T(128)S(1)} %copy-done.91, f32[8,128,32]{1,2,0:T(8,128)S(1)} %copy-done.29, f32[8,128,32]{1,2,0:T(8,128)S(1)} %bitcast.300, f32[8,128,32]{1,2,0:T(8,128)S(1)} %copy-done.37, ...), kind=kOutput, calls=%fused_computation.58 | convolution fusion | flops 3250585600 | bytes 34488448 | tf_op jit(solution)/shard_map/transpose(jvp(bijh,bjhp->bihp))/dot_general | solution.py:69
  535.7 36.3 %while.31 = (s32[]{:T(128)}, f32[8,32]{1,0:T(8,128)}, f32[32,8,8]{2,1,0:T(8,128)S(1)}, f32[8,32,8,8]{3,2,1,0:T(8,128)}, s32[8]{0:T(128)}, /*index=5*/f32[8,32]{0...) while((s32[]{:T(128)}, f32[8,32]{1,0:T(8,128)}, f32[32,8,8]{2,1,0:T(8,128)S(1)}, ...), condition=%wide.region_15.16_spmd.clone, body=%wide.region_14.15_spmd.clone.sunk | while | flops 420484 | bytes 210855 | solution.py:48
  580.5 9.2 copy.170
  589.8 18.6 %multiply_reduce_fusion.6 = (f32[2048]{0:T(1024)}, f32[2048]{0:T(1024)}, f32[2048]{0:T(1024)}, f32[2048]{0:T(1024)}, f32[2048]{0:T(1024)}, /*index=5*/f32[8,128,2048]{2,1,0:T(8,128)S(1)}) fusion(f32[8,128,2048]{2,1,0:T(8,128)} %copy-done.7, f32[8,3,2048]{2,1,0:T(4,128)S(1)} %copy-done.19, f32[8,128,2048]{2,1,0:T(8,128)} %get-tuple-element.379, ...), kind=kLoop, calls=%fused_computation.74 | loop fusion | flops 44029952 | bytes 33792000 | tf_op jit(solution)/shard_map/transpose(jvp())/reduce_sum | solution.py:31
  608.4 11.9 broadcast_multiply_fusion
  628.8 13.1 pad_add_fusion
  649.8 15.6 %fusion.87 = f32[1024,2048]{1,0:T(8,128)} fusion(bf16[1024,2048]{1,0:T(8,128)(2,1)S(1)} %copy-done.15, bf16[2048,1,2048]{2,1,0:T(2,128)(2,1)} %get-tuple-element.381), kind=kOutput, calls=%fused_computation.142 | convolution fusion | flops 8589934592 | bytes 20971520 | tf_op jit(solution)/shard_map/dot_general | solution.py:97
  665.4 24.1 %multiply_reduce_fusion.8 = (f32[2048]{0:T(1024)S(1)}, bf16[1024,2048]{1,0:T(8,128)(2,1)}, bf16[1024,2048]{1,0:T(8,128)(2,1)}) fusion(bf16[1024,2048]{1,0:T(8,128)(2,1)} %param.18, f32[1024]{0:T(1024)S(1)} %copy-done.59, bf16[1024,2048]{1,0:T(8,128)(2,1)} %all-reduce.30.cloned.1.call-done, f32[1024,2048]{1,0:T(8,128)} %fusion.138, ...), kind=kOutput, calls=%fused_computation.78 | convolution fusion | flops 8613001216 | bytes 54538240 | tf_op jit(solution)/shard_map/dot_general | solution.py:97
  698.6 15.2 %convolution_convert_fusion = bf16[2048,2048]{1,0:T(8,128)(2,1)} fusion(bf16[1024,2048]{1,0:T(8,128)(2,1)} %param.30, f32[1024,2048]{1,0:T(8,128)} %get-tuple-element.375, f32[2048]{0:T(1024)S(1)} %copy-done.74, f32[1024]{0:T(1024)S(1)} %copy-done.62), kind=kOutput, calls=%fused_computation.125 | convolution fusion | flops 8600420352 | bytes 20983808 | tf_op jit(solution)/shard_map/dot_general | solution.py:91
  713.8 12.4 copy.213
  732.8 12.8 reduce-scatter.9.cloned.1.call-done
  755.1 12.7 convert_bitcast_fusion.1
  767.8 9.8 convert_bitcast_fusion.2
  777.6 6.8 pad_maximum_fusion
  784.6 26.8 %all-reduce.32.cloned.1.call-done = f32[2048,256]{1,0:T(8,128)} async-done(((f32[2048,256]{1,0:T(8,128)}), f32[2048,256]{1,0:T(8,128)}) %all-reduce.32.cloned.1.call-update) | async-done | bytes 2097168 | tf_op jit(solution)/shard_map/psum | solution.py:12
  811.9 59.8 %reduce-scatter.13.cloned.1.call-done = bf16[128,32]{1,0:T(8,128)(2,1)} async-done(((bf16[2048,32]{1,0:T(8,128)(2,1)}), bf16[128,32]{1,0:T(8,128)(2,1)}) %reduce-scatter.13.cloned.1.call-update) | async-done | bytes 8208
  873.1 8.1 all-reduce.25
  881.2 62.2 %all-reduce.24 = (f32[2048]{0:T(1024)}, f32[5,2048]{1,0:T(8,128)}, f32[5,256]{1,0:T(8,128)}, f32[32]{0:T(128)}, f32[32]{0:T(128)}, /*index=5*/f32[32]{0:T(128)}, f32[2048]{0:T(1024)}) all-reduce(f32[2048]{0:T(1024)S(1)} %get-tuple-element.362, f32[5,2048]{1,0:T(8,128)S(1)} %pad_add_fusion.3, ...), channel_id=1, replica_groups=mesh['dp'=16,'tensor'=2] {'dp'}, use_global_device_ids=true, to_apply=%region_24.25 | all-reduce | flops 15712 | bytes 125696 | tf_op jit(solution)/shard_map/psum | solution.py:12
  943.4 36.4 %reduce-scatter.15.cloned.1.call-done = bf16[128,2048]{1,0:T(8,128)(2,1)} async-done(((bf16[2048,2048]{1,0:T(8,128)(2,1)}), bf16[128,2048]{1,0:T(8,128)(2,1)}) %reduce-scatter.15.cloned.1.call-update) | async-done | bytes 524304
  982.2 56.2 %all-gather.2.cloned.1.call-done = bf16[1024,2048]{1,0:T(8,128)(2,1)} async-done(((bf16[512,2048]{1,0:T(8,128)(2,1)}), bf16[1024,2048]{1,0:T(8,128)(2,1)}) %all-gather.2.cloned.1.call-update) | async-done | bytes 4194320 | tf_op jit(solution)/shard_map/all_gather | solution.py:198
  1038.4 182.7 %reduce-scatter.11.cloned.1.call-done = bf16[128,2,2048]{2,0,1:T(8,128)(2,1)} async-done(((bf16[2048,2,2048]{2,0,1:T(8,128)(2,1)}), bf16[128,2,2048]{2,0,1:T(8,128)(2,1)}) %reduce-scatter.11.cloned.1.call-update) | async-done | bytes 1048592 | tf_op jit(solution)/shard_map/reduce_scatter | solution.py:200
  1224.7 96.7 %all-reduce.34.cloned.1.call-done = f32[2048,256]{1,0:T(8,128)} async-done(((f32[2048,256]{1,0:T(8,128)}), f32[2048,256]{1,0:T(8,128)}) %all-reduce.34.cloned.1.call-update) | async-done | bytes 2097168 | tf_op jit(solution)/shard_map/psum | solution.py:12
  (398 shorter events, 196.4 us)
Async XLA Ops:
  7.2 137.3 %copy-start = (bf16[2048,256]{1,0:T(8,128)(2,1)S(1)}, bf16[2048,256]{1,0:T(8,128)(2,1)}, u32[]{:S(2)}) copy-start(bf16[2048,256]{1,0:T(8,128)(2,1)} %param.21) | copy-start | bytes 3145732
  7.2 658.2 %all-reduce.30.cloned.1.call-start = ((), (), s32[]{:S(2)}) async-start(), calls=%async_computation.4 | async-start | bytes 8388608 | tf_op jit(solution)/shard_map/psum | solution.py:164
  8.0 51.4 %copy-start.79 = (s32[8]{0:T(128)}, s32[8]{0:T(128)S(1)}, u32[]{:S(2)}) copy-start(s32[8]{0:T(128)S(1)} %broadcast_maximum_fusion) | copy-start | bytes 100
  8.6 140.0 %copy-start.76 = (pred[8]{0:T(512)(128)(4,1)}, pred[8]{0:T(512)(128)(4,1)S(1)}, u32[]{:S(2)}) copy-start(pred[8]{0:T(512)(128)(4,1)S(1)} %get-tuple-element.413) | copy-start | bytes 28
  11.7 32.9 %copy-start.58 = (f32[1024]{0:T(1024)}, f32[1024]{0:T(1024)S(1)}, u32[]{:S(2)}) copy-start(f32[1024]{0:T(1024)S(1)} %add_rsqrt_fusion.1) | copy-start | bytes 12292
  11.7 32.8 %copy-start.60 = (f32[5,2048]{1,0:T(8,128)S(1)}, f32[5,2048]{1,0:T(8,128)}, u32[]{:S(2)}) copy-start(f32[5,2048]{1,0:T(8,128)} %param.23) | copy-start | bytes 122884
  11.8 32.9 %copy-start.6 = (bf16[1024,2048]{1,0:T(8,128)(2,1)S(1)}, bf16[1024,2048]{1,0:T(8,128)(2,1)}, u32[]{:S(2)}) copy-start(bf16[1024,2048]{1,0:T(8,128)(2,1)} %param.18) | copy-start | bytes 12582916
  11.8 32.9 %copy-start.48 = (f32[2048]{0:T(1024)S(1)}, f32[2048]{0:T(1024)}, u32[]{:S(2)}) copy-start(f32[2048]{0:T(1024)} %param.19) | copy-start | bytes 24580
  44.6 18.8 %copy-start.40 = (f32[1,2048]{1,0:T(1,128)}, f32[1,2048]{1,0:T(1,128)S(1)}, u32[]{:S(2)}) copy-start(f32[1,2048]{1,0:T(1,128)S(1)} %get-tuple-element.404) | copy-start | bytes 24580
  93.1 35.0 %copy-start.51 = (s32[8]{0:T(128)S(1)}, s32[8]{0:T(128)}, u32[]{:S(2)}) copy-start(s32[8]{0:T(128)} %param.31) | copy-start | bytes 100
  99.5 29.3 %copy-start.88 = (f32[32]{0:T(128)}, f32[32]{0:T(128)S(1)}, u32[]{:S(2)}) copy-start(f32[32]{0:T(128)S(1)} %exponential_negate_fusion) | copy-start | bytes 388
  127.3 24.2 %copy-start.9 = (f32[8,128,32]{2,0,1:T(8,128)}, f32[8,128,32]{2,0,1:T(8,128)S(1)}, u32[]{:S(2)}) copy-start(f32[8,128,32]{2,0,1:T(8,128)S(1)} %fusion.171) | copy-start | bytes 393220
  127.3 24.2 %copy-start.50 = (f32[8,32]{1,0:T(8,128)}, f32[8,32]{1,0:T(8,128)S(1)}, u32[]{:S(2)}) copy-start(f32[8,32]{1,0:T(8,128)S(1)} %slice_bitcast_fusion) | copy-start | bytes 3076
  128.0 33.0 %copy-start.34 = (f32[8,8]{0,1:T(8,128)}, f32[8,8]{0,1:T(8,128)S(1)}, u32[]{:S(2)}) copy-start(f32[8,8]{0,1:T(8,128)S(1)} %fusion.143) | copy-start | bytes 772
  154.9 22.9 %copy-start.28 = (f32[8,128,32]{1,2,0:T(8,128)}, f32[8,128,32]{1,2,0:T(8,128)S(1)}, u32[]{:S(2)}) copy-start(f32[8,128,32]{1,2,0:T(8,128)S(1)} %copy.150) | copy-start | bytes 393220
  170.1 21.2 %copy-start.22 = (f32[8,32]{0,1:T(8,128)}, f32[8,32]{0,1:T(8,128)S(1)}, u32[]{:S(2)}) copy-start(f32[8,32]{0,1:T(8,128)S(1)} %get-tuple-element.597) | copy-start | bytes 3076
  207.6 24.9 %copy-start.30 = (f32[8,128,128]{2,1,0:T(8,128)}, f32[8,128,128]{2,1,0:T(8,128)S(1)}, u32[]{:S(2)}) copy-start(f32[8,128,128]{2,1,0:T(8,128)S(1)} %fusion.173) | copy-start | bytes 1572868
  263.5 25.6 %copy-start.73 = (f32[2048]{0:T(1024)S(1)}, f32[2048]{0:T(1024)}, u32[]{:S(2)}) copy-start(f32[2048]{0:T(1024)} %param.28) | copy-start | bytes 24580
  289.1 37.3 %copy-start.61 = (f32[1024]{0:T(1024)}, f32[1024]{0:T(1024)S(1)}, u32[]{:S(2)}) copy-start(f32[1024]{0:T(1024)S(1)} %add_rsqrt_fusion) | copy-start | bytes 12292
  304.4 441.2 %reduce-scatter.9.cloned.1.call-start = ((), (), s32[]{:S(2)}) async-start(), calls=%async_computation.5 | async-start | bytes 6291456 | tf_op jit(solution)/shard_map/reduce_scatter | solution.py:190
  368.3 22.0 %slice-start.2 = ((s8[8388608]{0:T(1024)(128)(4,1)}), s8[4194304]{0:T(1024)(128)(4,1)S(1)}, s32[]{:S(2)}) async-start(s8[8388608]{0:T(1024)(128)(4,1)} %bitcast.258), calls=%async_computation.14 | async-start | bytes 8388608
  418.5 28.6 %slice-start = ((s8[8388608]{0:T(1024)(128)(4,1)}), s8[4194304]{0:T(1024)(128)(4,1)S(1)}, s32[]{:S(2)}) async-start(s8[8388608]{0:T(1024)(128)(4,1)} %bitcast.256), calls=%async_computation.12 | async-start | bytes 8388608
  463.0 30.0 %copy-start.12 = (f32[1024,256]{1,0:T(8,128)S(1)}, f32[1024,256]{1,0:T(8,128)}, u32[]{:S(2)}) copy-start(f32[1024,256]{1,0:T(8,128)} %copy-done.11) | copy-start | bytes 3145732
  463.0 30.0 %copy-start.17 = (f32[8,128,256]{2,1,0:T(8,128)S(1)}, f32[8,128,256]{2,1,0:T(8,128)}, u32[]{:S(2)}) copy-start(f32[8,128,256]{2,1,0:T(8,128)} %get-tuple-element.377) | copy-start | bytes 3145732
  463.0 30.0 %copy-start.33 = (f32[8,3,256]{2,1,0:T(4,128)S(1)}, f32[8,3,256]{2,1,0:T(4,128)}, u32[]{:S(2)}) copy-start(f32[8,3,256]{2,1,0:T(4,128)} %copy-done.32) | copy-start | bytes 73732
  507.7 28.0 %copy-start.23 = (f32[8,32]{0,1:T(8,128)S(1)}, f32[8,32]{0,1:T(8,128)}, u32[]{:S(2)}) copy-start(f32[8,32]{0,1:T(8,128)} %copy-done.22) | copy-start | bytes 3076
  531.3 40.7 %copy-start.10 = (f32[8,128,32]{2,0,1:T(8,128)S(1)}, f32[8,128,32]{2,0,1:T(8,128)}, u32[]{:S(2)}) copy-start(f32[8,128,32]{2,0,1:T(8,128)} %copy-done.9) | copy-start | bytes 393220
  531.3 43.3 %copy-start.13 = (f32[8,128,32]{2,0,1:T(8,128)S(1)}, f32[8,128,32]{2,0,1:T(8,128)}, u32[]{:S(2)}) copy-start(f32[8,128,32]{2,0,1:T(8,128)} %copy.149) | copy-start | bytes 393220
  689.5 121.9 %all-reduce.32.cloned.1.call-start = ((), (), s32[]{:S(2)}) async-start(), calls=%async_computation.8 | async-start | bytes 4194304 | tf_op jit(solution)/shard_map/psum | solution.py:12
  694.4 177.2 %reduce-scatter.13.cloned.1.call-start = ((), (), s32[]{:S(2)}) async-start(), calls=%async_computation.10 | async-start | bytes 557056
  698.5 281.3 %reduce-scatter.15.cloned.1.call-start = ((), (), s32[]{:S(2)}) async-start(), calls=%async_computation.11 | async-start | bytes 8912896
  726.2 19.4 %copy-start.49 = (f32[2048]{0:T(1024)S(1)}, f32[2048]{0:T(1024)}, u32[]{:S(2)}) copy-start(f32[2048]{0:T(1024)} %param.19) | copy-start | bytes 24580
  726.2 312.1 %all-gather.2.cloned.1.call-start = ((), (), s32[]{:S(2)}) async-start(), calls=%async_computation.6 | async-start | bytes 6291456 | tf_op jit(solution)/shard_map/all_gather | solution.py:198
  755.0 466.0 %reduce-scatter.11.cloned.1.call-start = ((), (), s32[]{:S(2)}) async-start(), calls=%async_computation.7 | async-start | bytes 17825792 | tf_op jit(solution)/shard_map/reduce_scatter | solution.py:200
  784.5 27.0 %copy-start.52 = (f32[2048]{0:T(1024)S(1)}, f32[2048]{0:T(1024)}, u32[]{:S(2)}) copy-start(f32[2048]{0:T(1024)} %get-tuple-element.364) | copy-start | bytes 24580
  784.5 27.2 %copy-start.81 = (f32[256]{0:T(256)S(1)}, f32[256]{0:T(256)}, u32[]{:S(2)}) copy-start(f32[256]{0:T(256)} %get-tuple-element.326) | copy-start | bytes 3076
  784.5 27.2 %copy-start.82 = (f32[256]{0:T(256)S(1)}, f32[256]{0:T(256)}, u32[]{:S(2)}) copy-start(f32[256]{0:T(256)} %get-tuple-element.327) | copy-start | bytes 3076
  784.5 27.2 %copy-start.83 = (f32[256]{0:T(256)S(1)}, f32[256]{0:T(256)}, u32[]{:S(2)}) copy-start(f32[256]{0:T(256)} %get-tuple-element.328) | copy-start | bytes 3076
  784.5 27.2 %copy-start.84 = (f32[256]{0:T(256)S(1)}, f32[256]{0:T(256)}, u32[]{:S(2)}) copy-start(f32[256]{0:T(256)} %get-tuple-element.329) | copy-start | bytes 3076
  784.5 27.2 %copy-start.85 = (f32[256]{0:T(256)S(1)}, f32[256]{0:T(256)}, u32[]{:S(2)}) copy-start(f32[256]{0:T(256)} %get-tuple-element.330) | copy-start | bytes 3076
  784.5 27.3 %copy-start.93 = (f32[32]{0:T(128)S(1)}, f32[32]{0:T(128)}, u32[]{:S(2)}) copy-start(f32[32]{0:T(128)} %param.26) | copy-start | bytes 388
  784.5 27.3 %copy-start.53 = (f32[2048]{0:T(1024)S(1)}, f32[2048]{0:T(1024)}, u32[]{:S(2)}) copy-start(f32[2048]{0:T(1024)} %get-tuple-element.316) | copy-start | bytes 24580
  784.5 27.3 %copy-start.54 = (f32[2048]{0:T(1024)S(1)}, f32[2048]{0:T(1024)}, u32[]{:S(2)}) copy-start(f32[2048]{0:T(1024)} %get-tuple-element.317) | copy-start | bytes 24580
  784.5 27.3 %copy-start.55 = (f32[2048]{0:T(1024)S(1)}, f32[2048]{0:T(1024)}, u32[]{:S(2)}) copy-start(f32[2048]{0:T(1024)} %get-tuple-element.318) | copy-start | bytes 24580
  784.5 27.3 %copy-start.56 = (f32[2048]{0:T(1024)S(1)}, f32[2048]{0:T(1024)}, u32[]{:S(2)}) copy-start(f32[2048]{0:T(1024)} %get-tuple-element.321) | copy-start | bytes 24580
  784.5 27.3 %copy-start.57 = (f32[2048]{0:T(1024)S(1)}, f32[2048]{0:T(1024)}, u32[]{:S(2)}) copy-start(f32[2048]{0:T(1024)} %get-tuple-element.322) | copy-start | bytes 24580
  784.6 96.6 %copy-start.75 = (f32[2048]{0:T(1024)S(1)}, f32[2048]{0:T(1024)}, u32[]{:S(2)}) copy-start(f32[2048]{0:T(1024)} %get-tuple-element.319) | copy-start | bytes 24580
  784.6 536.8 %all-reduce.34.cloned.1.call-start = ((), (), s32[]{:S(2)}) async-start(), calls=%async_computation.9 | async-start | bytes 4194304 | tf_op jit(solution)/shard_map/psum | solution.py:12
  (58 other events, 583.1 us)
Sparse Core Ops, SparseCore 0:
  304.5 109.7 all-reduce.29
  689.6 55.9 reduce-scatter.8
  748.5 62.9 all-reduce.31
  815.9 55.7 reduce-scatter.12
  875.5 104.2 reduce-scatter.14
  981.8 56.5 all-gather.1
  1042.5 178.5 reduce-scatter.10
  1224.6 96.7 all-reduce.33
